TPU v7x, 512 devices: a whole 4x8x8 slice. The times are simulated.
512 devices in a mesh: row: 32 (over z, x), col: 16 (over y, core).
Axes of the slice: x: 4, y: 8, z: 8, core: 2. Of those that a mesh axis runs over, the one named last changes fastest.
Arguments:
- source_points: float32 [3, 65536], P(None, 'row'), may hold values from -4 to 4
- target_points: float32 [3, 262144], P(None, 'col'), may hold values from -4 to 4
- source_potential: float32 [65536], P('row'), may hold values from -2.5 to 3.6
- target_potential: float32 [262144], P('col'), may hold values from -2.5 to 3.6
- neighbours: int32 [256, 64], P('row'), may hold values from -1 to 1023, as said below
Outputs:
- source_dual: float32 [65536], P('row')
- target_dual: float32 [262144], P('col')
Inputs may be any that keep to these rules, and one draw needn't show every extreme that they name: `neighbours`: each row block lists, in increasing order, between 32 and 64 distinct column-block ids, then -1 up to 64 entries; some row block lists 64; every column block is listed by at least one row block.
All inputs are finite; a program needn't handle non-finite values.
Results may differ from a plain program's by a relative error of at most 0.0003.
Values sent between devices are 32-bit elements; how exact they have to be, the bound alone decides.
No kernel may reach another device: no remote copies, remote signals or barrier semaphores. Data moves between devices by JAX's collectives and lax.ppermute only.
A program may use at most 64 MiB of HBM per device.

v0:
```python
import functools
import math

import jax
import jax.numpy as jnp
from jax import lax
from jax.experimental import pallas as pl
from jax.experimental.pallas import tpu as pltpu
from jax.sharding import PartitionSpec as P


BLOCK = 256
EPS = 0.02
SCALE = math.log2(math.e) / EPS
BACK = -EPS * math.log(2.0)
NEG = -1e30
LANES = 128
TURN = 4
F32 = jnp.float32


def split(values):
    first = values.astype(jnp.bfloat16).astype(F32)
    rest = values - first
    second = rest.astype(jnp.bfloat16).astype(F32)
    third = (rest - second).astype(jnp.bfloat16).astype(F32)
    return first, second, third


def factors(values, streamed):
    first, second, third = split(values)
    if streamed:
        rows = (first, second, first, second, third, first)
    else:
        rows = (first, first, second, second, first, third)
    none = jnp.zeros_like(first)
    return jnp.concatenate((*rows, none, none), axis=0).astype(jnp.bfloat16)


def half_norm(points):
    return 0.5 * (points[0:1] * points[0:1] + points[1:2] * points[1:2] + points[2:3] * points[2:3])


def with_level(points, level):
    return jnp.concatenate((SCALE * points, SCALE * (level - half_norm(points))), axis=0)


def with_one(points):
    return jnp.concatenate((points, jnp.ones_like(points[0:1])), axis=0)


def span(lists, row, lo, size):
    width = lists.shape[1]

    def before(bound):
        at = jnp.int32(0)
        steps = [width >> s for s in range(1, width.bit_length())] + [1]
        for step in steps:
            value = lists[row, at + (step - 1)]
            at = at + jnp.where((value >= 0) & (value < bound), step, 0)
        return at

    start = before(lo)
    return start, before(lo + size) - start


def tops(block):
    return jnp.max(block.reshape(-1, 8, block.shape[-1]), axis=0)


def joined(top, mass):
    peak = jnp.max(top, axis=0, keepdims=True)
    total = jnp.sum(mass * jnp.exp2(top - peak), axis=0, keepdims=True)
    return jnp.where(total > 0, peak + jnp.log2(total), NEG)


def listed(lists, codes, lo, size):
    spans = [span(lists, row, lo, size) for row in range(lists.shape[0])]
    codes[0] = 0
    total = jnp.int32(0)
    for row, (start, count) in enumerate(spans):

        def put(turn, _, row=row, start=start, total=total):
            value = lists[row, start + turn] - lo
            codes[total + turn] = row * size + jnp.clip(value, 0, size - 1)
            return 0

        lax.fori_loop(0, count, put, 0)
        total = total + count
    codes[codes.shape[0] - 1] = total


def pair_loop(codes, size, chunk, product, place, tops_ref, mass_ref, bufs, peaks):
    count = codes[codes.shape[0] - 1]
    last = jnp.maximum(count - 1, 0)
    shift = size.bit_length() - 1
    each = len(bufs) // 2

    def pair(turn):
        code = codes[jnp.minimum(turn, last)]
        return code >> shift, code & (size - 1)

    def fill(turn, slot):
        row, column = pair(turn)
        peak = None
        for at in range(0, BLOCK, chunk):
            part = product(row, column, at, chunk)
            bufs[slot][at : at + chunk] = part
            here = tops(part)
            peak = here if peak is None else jnp.maximum(peak, here)
        peaks[slot][...] = peak

    def absorb(turn, slot, sure):
        k = place(*pair(turn))
        top = tops_ref[k]
        new = jnp.maximum(top, peaks[slot][...])
        mass = None
        for at in range(0, BLOCK, chunk):
            part = bufs[slot][at : at + chunk].reshape(-1, 8, BLOCK)
            here = jnp.sum(jnp.exp2(part - new[None]), axis=0)
            mass = here if mass is None else mass + here
        if not sure:
            mass = jnp.where(turn < count, mass, 0.0)
        mass_ref[k] = mass_ref[k] * jnp.exp2(top - new) + mass
        tops_ref[k] = new

    for slot in range(each):
        fill(slot, slot)

    def turns(step, _):
        turn = 2 * each * step
        for slot in range(each):
            fill(turn + each + slot, each + slot)
            absorb(turn + slot, slot, slot == 0)
        for slot in range(each):
            fill(turn + 2 * each + slot, slot)
            absorb(turn + each + slot, each + slot, False)
        return 0

    lax.fori_loop(0, (count + 2 * each - 1) // (2 * each), turns, 0)


def cleared(tops_ref, mass_ref, k):
    tops_ref[k] = jnp.full(tops_ref.shape[1:], NEG, F32)
    mass_ref[k] = jnp.zeros(mass_ref.shape[1:], F32)


def row_kernel(codes, source, target, level, out, left, right, tops_ref, mass_ref, *work):
    block = BLOCK
    wide = block // LANES
    rows = source.shape[1] // block
    size = target.shape[1] // block
    for b in range(rows):
        right[b] = factors(with_one(source[:, b * block : (b + 1) * block]), False)
        cleared(tops_ref, mass_ref, b)

    def build(k, _):
        at = pl.ds(pl.multiple_of(k * block, block), block)
        left[k] = factors(with_level(target[:, at], level[:, at]), True)
        return 0

    lax.fori_loop(0, size, build, 0, unroll=4)

    def product(row, column, at, chunk):
        return lax.dot_general(
            left[column][:, at : at + chunk],
            right[row],
            (((0,), (0,)), ((), ())),
            preferred_element_type=F32,
        )

    half = len(work) // 2
    pair_loop(
        codes, size, 128, product, lambda row, column: row, tops_ref, mass_ref, work[:half], work[half:]
    )
    for b in range(rows):
        line = joined(tops_ref[b], mass_ref[b]) - SCALE * half_norm(
            source[:, b * block : (b + 1) * block]
        )
        for part in range(wide):
            piece = line[:, part * LANES : (part + 1) * LANES]
            out[:, b * wide + part : b * wide + part + 1, :] = jnp.broadcast_to(
                piece[None], (out.shape[0], 1, LANES)
            )


def new_level(pieces, old):
    peak = jnp.max(pieces, axis=0)
    total = jnp.sum(jnp.exp2(pieces - peak[None]), axis=0)
    return 0.5 * (old + BACK * (peak + jnp.log2(total)))


def column_kernel(fresh, source, target, level, *rest):
    if fresh:
        column, lists, out, codes, left, right, tops_ref, mass_ref, *work = rest
        now = level[...]
        listed(lists, codes, column[0] * right.shape[0], right.shape[0])
    else:
        codes, pieces, out, level_out, left, right, tops_ref, mass_ref, *work = rest
        now = new_level(pieces[...], level[...])
        level_out[...] = now
    block = BLOCK
    wide = block // LANES
    rows = source.shape[1] // block
    size = target.shape[1] // block
    for b in range(rows):
        line = jnp.concatenate(
            [now[b * wide + part : b * wide + part + 1] for part in range(wide)], axis=1
        )
        here = factors(with_level(source[:, b * block : (b + 1) * block], line), True)
        left[b] = here.astype(F32).T.astype(jnp.bfloat16)

    def build(k, _):
        at = pl.ds(pl.multiple_of(k * block, block), block)
        right[k] = factors(with_one(target[:, at]), False)
        cleared(tops_ref, mass_ref, k)
        return 0

    lax.fori_loop(0, size, build, 0, unroll=4)

    def product(row, column, at, chunk):
        return jnp.dot(left[row][at : at + chunk], right[column], preferred_element_type=F32)

    half = len(work) // 2
    pair_loop(
        codes, size, 64, product, lambda row, column: column, tops_ref, mass_ref, work[:half], work[half:]
    )
    each = size // out.shape[0]

    def finish(piece, _):
        for e in range(each):
            k = piece * each + e
            at = pl.ds(pl.multiple_of(k * block, block), block)
            line = joined(tops_ref[k], mass_ref[k]) - SCALE * half_norm(target[:, at])
            for part in range(wide):
                out[piece, e * wide + part : e * wide + part + 1, :] = line[
                    :, part * LANES : (part + 1) * LANES
                ]
        return 0

    lax.fori_loop(0, out.shape[0], finish, 0, unroll=4)


def combine_kernel(place_ref, pieces, level, out):
    out[...] = jnp.broadcast_to(new_level(pieces[...], level[place_ref[0]])[None], out.shape)


def last_kernel(pieces, level, out):
    out[...] = new_level(pieces[...], level[...])


SMEM = pl.BlockSpec(memory_space=pltpu.SMEM)
VMEM = pl.BlockSpec(memory_space=pltpu.VMEM)


def call(body, outs, ins, scratch=(), limit=24 << 20):
    several = isinstance(outs, list)
    shapes = outs if several else [outs]
    shaped = [s if isinstance(s, jax.ShapeDtypeStruct) else jax.ShapeDtypeStruct(s, F32) for s in shapes]
    specs = [SMEM if s.dtype == jnp.int32 else VMEM for s in shaped]
    return pl.pallas_call(
        body,
        out_shape=shaped if several else shaped[0],
        in_specs=ins,
        out_specs=specs if several else specs[0],
        scratch_shapes=list(scratch),
        compiler_params=pltpu.CompilerParams(vmem_limit_bytes=limit),
    )


def scratch(left, right, places):
    return [
        pltpu.VMEM(left, jnp.bfloat16),
        pltpu.VMEM(right, jnp.bfloat16),
        *[pltpu.VMEM((places, 8, BLOCK), F32)] * 2,
        *[pltpu.VMEM((BLOCK, BLOCK), F32)] * (2 * TURN),
        *[pltpu.VMEM((8, BLOCK), F32)] * (2 * TURN),
    ]


def exchanged(array, axis):
    return lax.all_to_all(array, axis, 0, 0, tiled=True)


def on_device(source_points, target_points, source_potential, target_potential, neighbours):
    n_row = lax.axis_size("row")
    n_col = lax.axis_size("col")
    rows = source_points.shape[1] // BLOCK
    size = target_points.shape[1] // BLOCK
    col = lax.axis_index("col").astype(jnp.int32).reshape(1)
    row = lax.axis_index("row").astype(jnp.int32).reshape(1)
    source_lines = source_points.shape[1] // LANES
    share = target_points.shape[1] // LANES // n_row
    source_level = source_potential.reshape(source_lines, LANES)
    target_level = target_potential.reshape(n_row, share, LANES)
    codes_shape = jax.ShapeDtypeStruct((neighbours.size + LANES,), jnp.int32)
    column_scratch = scratch((rows, BLOCK, 32), (size, 32, BLOCK), size)
    row_scratch = scratch((size, 32, BLOCK), (rows, 32, BLOCK), rows)
    column_out = (n_row, share, LANES)
    row_out = (n_col, source_lines, LANES)

    def row_phase(codes, level):
        return call(row_kernel, row_out, [SMEM, VMEM, VMEM, VMEM], row_scratch)(
            codes, source_points, target_points, level.reshape(1, -1)
        )

    def column_level(pieces, level):
        spread = call(combine_kernel, pieces.shape, [SMEM, VMEM, VMEM], ())(row, pieces, level)
        return exchanged(spread, "row")

    columns_0, codes = call(
        functools.partial(column_kernel, True),
        [column_out, codes_shape],
        [VMEM, VMEM, VMEM, SMEM, SMEM],
        column_scratch,
        60 << 20,
    )(source_points, target_points, source_level, col, neighbours)
    column_pieces_0 = exchanged(columns_0, "row")
    row_pieces_0 = exchanged(row_phase(codes, target_level), "col")
    target_1 = column_level(column_pieces_0, target_level)
    columns_1, source_1 = call(
        functools.partial(column_kernel, False),
        [column_out, source_level.shape],
        [VMEM, VMEM, VMEM, SMEM, VMEM],
        column_scratch,
    )(source_points, target_points, source_level, codes, row_pieces_0)
    column_pieces_1 = exchanged(columns_1, "row")
    rows_1 = row_phase(codes, target_1)
    column_pieces_1, rows_1 = lax.optimization_barrier((column_pieces_1, rows_1))
    row_pieces_1 = exchanged(rows_1, "col")
    spread = call(combine_kernel, column_out, [SMEM, VMEM, VMEM], ())(row, column_pieces_1, target_1)
    target_2 = exchanged(spread, "row")
    source_2 = call(last_kernel, source_level.shape, [VMEM, VMEM], ())(
        row_pieces_1, source_1
    )
    return source_2.reshape(-1), target_2.reshape(-1)


def solution(mesh):
    in_specs = (P(None, "row"), P(None, "col"), P("row"), P("col"), P("row", None))
    return jax.shard_map(
        on_device, mesh=mesh, in_specs=in_specs, out_specs=(P("row"), P("col")), check_vma=False
    )
```

profile of v0, /device:TPU:1, one launch (start us, length us, event | category | flops | bytes accessed | tf_op | source)
XLA Modules:
  0.0 120.2 jit_solution(15729800845692332790)
XLA Ops:
  0.6 0.0 copy-start
  0.6 3.5 %shard_map.68 = (f32[32,4,128]{2,1,0:T(4,128)}, s32[640]{0:T(1024)}) custom-call(f32[3,2048]{1,0:T(4,128)} %source.7, f32[3,16384]{1,0:T(4,128)} %target.7, f32[16,128]{1,0:T(8,128)} %bitcast.11, s32[1]{0:T(128)} %bitcast.1.rest_0_, s32[8,64]{1,0:T(8,128)} %rest_1_.1), custom_call_target="tpu_custom_call" | custom-call | tf_op jit(solution)/shard_map/pallas_call | solution.py:311
  4.2 0.0 copy-start.1
  4.2 0.0 copy-start.2
  4.2 0.0 copy-start.3
  4.2 13.8 %all-to-all-start.2 = ((f32[32,4,128]{2,1,0:T(4,128)}), f32[32,4,128]{2,1,0:T(4,128)S(1)}, u32[]{:S(2)}, u32[]{:S(2)}) async-start(f32[32,4,128]{2,1,0:T(4,128)} %get-tuple-element.10), calls=%async_computation.2 | async-start | bytes 131072 | tf_op jit(solution)/shard_map/all_to_all | solution.py:282
  18.0 0.0 copy-done
  18.1 0.0 copy-done.1
  18.1 0.0 copy-done.2
  18.1 0.0 copy-done.3
  18.1 2.2 %shard_map.69 = f32[16,16,128]{2,1,0:T(8,128)} custom-call(s32[640]{0:T(1024)S(1)} %copy-done.3, f32[3,2048]{1,0:T(4,128)S(1)} %copy-done.1, f32[3,16384]{1,0:T(4,128)S(1)} %copy-done, f32[1,16384]{1,0:T(1,128)S(1)} %bitcast.9), custom_call_target="tpu_custom_call" | custom-call | tf_op jit(solution)/shard_map/pallas_call | solution.py:303
  20.3 6.6 %all-to-all-done.2.pieces = f32[32,4,128]{2,1,0:T(4,128)S(1)} async-done(((f32[32,4,128]{2,1,0:T(4,128)}), f32[32,4,128]{2,1,0:T(4,128)S(1)}, u32[]{:S(2)}, u32[]{:S(2)}) %all-to-all-start.2) | async-done | bytes 65568 | tf_op jit(solution)/shard_map/all_to_all | solution.py:282
  26.9 14.9 %all-to-all-start = ((f32[16,16,128]{2,1,0:T(8,128)}), f32[16,16,128]{2,1,0:T(8,128)S(1)}, u32[]{:S(2)}, u32[]{:S(2)}) async-start(f32[16,16,128]{2,1,0:T(8,128)} %shard_map.69), calls=%async_computation | async-start | bytes 262144 | tf_op jit(solution)/shard_map/all_to_all | solution.py:282
  41.8 0.7 shard_map.71
  42.5 0.0 copy-start.4
  42.5 8.2 %all-to-all-done.rest_1_ = f32[16,16,128]{2,1,0:T(8,128)S(1)} async-done(((f32[16,16,128]{2,1,0:T(8,128)}), f32[16,16,128]{2,1,0:T(8,128)S(1)}, u32[]{:S(2)}, u32[]{:S(2)}) %all-to-all-start) | async-done | bytes 131104 | tf_op jit(solution)/shard_map/all_to_all | solution.py:282
  50.7 9.0 %all-to-all-start.3 = ((f32[32,4,128]{2,1,0:T(4,128)}), f32[32,4,128]{2,1,0:T(4,128)S(1)}, u32[]{:S(2)}, u32[]{:S(2)}) async-start(f32[32,4,128]{2,1,0:T(4,128)} %shard_map.71), calls=%async_computation.3 | async-start | bytes 131072 | tf_op jit(solution)/shard_map/all_to_all | solution.py:282
  59.7 0.0 copy-done.4
  59.7 2.7 %shard_map.70 = (f32[32,4,128]{2,1,0:T(4,128)}, f32[16,128]{1,0:T(8,128)S(1)}) custom-call(f32[3,2048]{1,0:T(4,128)S(1)} %copy-done.1, f32[3,16384]{1,0:T(4,128)S(1)} %copy-done, f32[16,128]{1,0:T(8,128)S(1)} %bitcast.12, s32[640]{0:T(1024)S(1)} %copy-done.3, f32[16,16,128]{2,1,0:T(8,128)S(1)} %all-to-all-done.rest_1_), custom_call_target="tpu_custom_call" | custom-call | tf_op jit(solution)/shard_map/pallas_call | solution.py:321
  62.4 6.1 %all-to-all-done.3.level = f32[32,4,128]{2,1,0:T(4,128)S(1)} async-done(((f32[32,4,128]{2,1,0:T(4,128)}), f32[32,4,128]{2,1,0:T(4,128)S(1)}, u32[]{:S(2)}, u32[]{:S(2)}) %all-to-all-start.3) | async-done | bytes 65568 | tf_op jit(solution)/shard_map/all_to_all | solution.py:282
  68.5 3.8 %all-to-all-start.1 = ((f32[32,4,128]{2,1,0:T(4,128)}), f32[32,4,128]{2,1,0:T(4,128)S(1)}, u32[]{:S(2)}, u32[]{:S(2)}) async-start(f32[32,4,128]{2,1,0:T(4,128)} %get-tuple-element.9), calls=%async_computation.1 | async-start | bytes 131072 | tf_op jit(solution)/shard_map/all_to_all | solution.py:282
  72.4 2.2 %shard_map.72 = f32[16,16,128]{2,1,0:T(8,128)} custom-call(s32[640]{0:T(1024)S(1)} %copy-done.3, f32[3,2048]{1,0:T(4,128)S(1)} %copy-done.1, f32[3,16384]{1,0:T(4,128)S(1)} %copy-done, f32[1,16384]{1,0:T(1,128)S(1)} %bitcast.8), custom_call_target="tpu_custom_call" | custom-call | tf_op jit(solution)/shard_map/pallas_call | solution.py:303
  74.6 6.7 %all-to-all-done.1.pieces = f32[32,4,128]{2,1,0:T(4,128)S(1)} async-done(((f32[32,4,128]{2,1,0:T(4,128)}), f32[32,4,128]{2,1,0:T(4,128)S(1)}, u32[]{:S(2)}, u32[]{:S(2)}) %all-to-all-start.1) | async-done | bytes 65568 | tf_op jit(solution)/shard_map/all_to_all | solution.py:282
  81.2 0.1 shard_map.74
  81.3 11.9 %all_to_all.30 = f32[32,4,128]{2,1,0:T(4,128)S(1)} all-to-all(f32[32,4,128]{2,1,0:T(4,128)S(1)} %shard_map.74), channel_id=1, replica_groups=mesh['row'=32,'col'=16] {'row'}, dimensions={0} | all-to-all | bytes 131072 | tf_op jit(solution)/shard_map/all_to_all | solution.py:282
  93.2 16.8 %all-to-all-start.4 = ((f32[16,16,128]{2,1,0:T(8,128)}), f32[16,16,128]{2,1,0:T(8,128)S(1)}, u32[]{:S(2)}, u32[]{:S(2)}) async-start(f32[16,16,128]{2,1,0:T(8,128)} %shard_map.72), calls=%async_computation.4 | async-start | bytes 262144 | tf_op jit(solution)/shard_map/all_to_all | solution.py:282
  110.0 8.9 %all-to-all-done.4.pieces = f32[16,16,128]{2,1,0:T(8,128)S(1)} async-done(((f32[16,16,128]{2,1,0:T(8,128)}), f32[16,16,128]{2,1,0:T(8,128)S(1)}, u32[]{:S(2)}, u32[]{:S(2)}) %all-to-all-start.4) | async-done | bytes 131104 | tf_op jit(solution)/shard_map/all_to_all | solution.py:282
  118.9 0.6 shard_map.73
  119.5 0.6 copy.8
Async XLA Ops:
  0.6 17.4 %copy-start = (f32[3,16384]{1,0:T(4,128)S(1)}, f32[3,16384]{1,0:T(4,128)}, u32[]{:S(2)}) copy-start(f32[3,16384]{1,0:T(4,128)} %target.7) | copy-start | bytes 589828
  4.2 13.9 %copy-start.1 = (f32[3,2048]{1,0:T(4,128)S(1)}, f32[3,2048]{1,0:T(4,128)}, u32[]{:S(2)}) copy-start(f32[3,2048]{1,0:T(4,128)} %source.7) | copy-start | bytes 73732
  4.2 13.9 %copy-start.2 = (f32[16384]{0:T(1024)S(1)}, f32[16384]{0:T(1024)}, u32[]{:S(2)}) copy-start(f32[16384]{0:T(1024)} %param.8) | copy-start | bytes 196612
  4.2 13.9 %copy-start.3 = (s32[640]{0:T(1024)S(1)}, s32[640]{0:T(1024)}, u32[]{:S(2)}) copy-start(s32[640]{0:T(1024)} %get-tuple-element.8.codes.rest_0_) | copy-start | bytes 7684
  4.2 22.7 %all-to-all-start.2 = ((f32[32,4,128]{2,1,0:T(4,128)}), f32[32,4,128]{2,1,0:T(4,128)S(1)}, u32[]{:S(2)}, u32[]{:S(2)}) async-start(f32[32,4,128]{2,1,0:T(4,128)} %get-tuple-element.10), calls=%async_computation.2 | async-start | bytes 131072 | tf_op jit(solution)/shard_map/all_to_all | solution.py:282
  26.9 23.8 %all-to-all-start = ((f32[16,16,128]{2,1,0:T(8,128)}), f32[16,16,128]{2,1,0:T(8,128)S(1)}, u32[]{:S(2)}, u32[]{:S(2)}) async-start(f32[16,16,128]{2,1,0:T(8,128)} %shard_map.69), calls=%async_computation | async-start | bytes 262144 | tf_op jit(solution)/shard_map/all_to_all | solution.py:282
  42.5 17.2 %copy-start.4 = (f32[2048]{0:T(1024)S(1)}, f32[2048]{0:T(1024)}, u32[]{:S(2)}) copy-start(f32[2048]{0:T(1024)} %param.7) | copy-start | bytes 24580
  50.7 17.9 %all-to-all-start.3 = ((f32[32,4,128]{2,1,0:T(4,128)}), f32[32,4,128]{2,1,0:T(4,128)S(1)}, u32[]{:S(2)}, u32[]{:S(2)}) async-start(f32[32,4,128]{2,1,0:T(4,128)} %shard_map.71), calls=%async_computation.3 | async-start | bytes 131072 | tf_op jit(solution)/shard_map/all_to_all | solution.py:282
  68.5 12.7 %all-to-all-start.1 = ((f32[32,4,128]{2,1,0:T(4,128)}), f32[32,4,128]{2,1,0:T(4,128)S(1)}, u32[]{:S(2)}, u32[]{:S(2)}) async-start(f32[32,4,128]{2,1,0:T(4,128)} %get-tuple-element.9), calls=%async_computation.1 | async-start | bytes 131072 | tf_op jit(solution)/shard_map/all_to_all | solution.py:282
  93.2 25.7 %all-to-all-start.4 = ((f32[16,16,128]{2,1,0:T(8,128)}), f32[16,16,128]{2,1,0:T(8,128)S(1)}, u32[]{:S(2)}, u32[]{:S(2)}) async-start(f32[16,16,128]{2,1,0:T(8,128)} %shard_map.72), calls=%async_computation.4 | async-start | bytes 262144 | tf_op jit(solution)/shard_map/all_to_all | solution.py:282
where the time goes:
time: 121 us; the launch traced here: 120 us
  starting transfers between devices  58.4 us (48%)
  waiting for transfers between devices  36.4 us (30%)
  Pallas kernels  12 us (10%)
  blocking collectives  11.9 us (10%)
    all_to_all x5, starting transfers between devices, exchanged(): return lax.all_to_all(array, axis, 0, 0, tiled=True)  58.4 us
    all_to_all x5, waiting for transfers between devices, exchanged(): return lax.all_to_all(array, axis, 0, 0, tiled=True)  36.4 us
    all_to_all x1, blocking collectives, exchanged(): return lax.all_to_all(array, axis, 0, 0, tiled=True)  11.9 us
    pallas_call x2, Pallas kernels, row_phase(): call(row_kernel, row_out, [SMEM, VMEM, VMEM, VMEM], row_scratch)  4.44 us
    pallas_call x1, Pallas kernels, on_device(): call(functools.partial(column_kernel, True), [column_out, codes_shape], [...  3.51 us
    pallas_call x1, Pallas kernels, on_device(): call(functools.partial(column_kernel, False), [column_out, source_level.s...  2.69 us
  transfers between devices with their start and end apart: 5, of which 5 were waited for; matrix products, arithmetic and copies ran while one was open for 0% of the time, Pallas kernels for 7%

commit v1 on v0

--- a/solution.py
+++ b/solution.py
@@ -6,6 +6,7 @@
 from jax import lax
 from jax.experimental import pallas as pl
 from jax.experimental.pallas import tpu as pltpu
+from jax.sharding import Mesh
 from jax.sharding import PartitionSpec as P
 
 
@@ -74,30 +75,37 @@
     return jnp.where(total > 0, peak + jnp.log2(total), NEG)
 
 
-def listed(lists, codes, lo, size):
-    spans = [span(lists, row, lo, size) for row in range(lists.shape[0])]
+def list_kernel(place, lists, codes):
+    size = place[2]
+    core = place[1]
+    lo = place[0] * 2 * size
+    spans = [span(lists, row, lo, 2 * size) for row in range(lists.shape[0])]
     codes[0] = 0
     total = jnp.int32(0)
     for row, (start, count) in enumerate(spans):
 
         def put(turn, _, row=row, start=start, total=total):
-            value = lists[row, start + turn] - lo
-            codes[total + turn] = row * size + jnp.clip(value, 0, size - 1)
+            value = jnp.clip(lists[row, start + turn] - lo, 0, 2 * size - 1)
+            codes[total + turn] = row * 2 * size + (value ^ (core * size))
             return 0
 
         lax.fori_loop(0, count, put, 0)
         total = total + count
-    codes[codes.shape[0] - 1] = total
+    half = (total + 1) // 2
+    mine = jnp.clip(total - core * half, 0, half)
+    codes[codes.shape[0] - 1] = mine
+    codes[codes.shape[0] - 2] = jnp.where(mine > 0, core * half, 0)
 
 
 def pair_loop(codes, size, chunk, product, place, tops_ref, mass_ref, bufs, peaks):
     count = codes[codes.shape[0] - 1]
+    first = codes[codes.shape[0] - 2]
     last = jnp.maximum(count - 1, 0)
     shift = size.bit_length() - 1
     each = len(bufs) // 2
 
     def pair(turn):
-        code = codes[jnp.minimum(turn, last)]
+        code = codes[first + jnp.minimum(turn, last)]
         return code >> shift, code & (size - 1)
 
     def fill(turn, slot):
@@ -145,21 +153,44 @@
     mass_ref[k] = jnp.zeros(mass_ref.shape[1:], F32)
 
 
-def row_kernel(codes, source, target, level, out, left, right, tops_ref, mass_ref, *work):
+def wide_line(lines, first):
+    return jnp.concatenate(
+        [lines[first + part : first + part + 1] for part in range(BLOCK // LANES)], axis=1
+    )
+
+
+def row_kernel(later, place, codes, source, mine, other, *rest):
+    if later:
+        level, out, left, right, tops_ref, mass_ref, *work = rest
+    else:
+        level_mine, level_other, out, left, right, tops_ref, mass_ref, *work = rest
     block = BLOCK
     wide = block // LANES
     rows = source.shape[1] // block
-    size = target.shape[1] // block
+    size = mine.shape[1] // block
     for b in range(rows):
         right[b] = factors(with_one(source[:, b * block : (b + 1) * block]), False)
         cleared(tops_ref, mass_ref, b)
-
-    def build(k, _):
-        at = pl.ds(pl.multiple_of(k * block, block), block)
-        left[k] = factors(with_level(target[:, at], level[:, at]), True)
-        return 0
-
-    lax.fori_loop(0, size, build, 0, unroll=4)
+    pieces = (level if later else level_mine).shape[0]
+    each = size // pieces
+    core = place[1]
+    for side, points in enumerate((mine, other)):
+
+        def build(piece, _, side=side, points=points):
+            if later:
+                lines = level[piece, core ^ side]
+            else:
+                lines = (level_mine, level_other)[side][piece]
+            for e in range(each):
+                k = piece * each + e
+                at = pl.ds(pl.multiple_of(k * block, block), block)
+                left[side * size + k] = factors(
+                    with_level(points[:, at], wide_line(lines, e * wide)), True
+                )
+            return 0
+
+        lax.fori_loop(0, pieces, build, 0, unroll=2)
+    size = 2 * size
 
     def product(row, column, at, chunk):
         return lax.dot_general(
@@ -190,59 +221,64 @@
     return 0.5 * (old + BACK * (peak + jnp.log2(total)))
 
 
-def column_kernel(fresh, source, target, level, *rest):
+def column_kernel(fresh, place, codes, source, mine, other, level, *rest):
     if fresh:
-        column, lists, out, codes, left, right, tops_ref, mass_ref, *work = rest
+        out, left, right, tops_ref, mass_ref, *work = rest
         now = level[...]
-        listed(lists, codes, column[0] * right.shape[0], right.shape[0])
     else:
-        codes, pieces, out, level_out, left, right, tops_ref, mass_ref, *work = rest
+        pieces, out, level_out, left, right, tops_ref, mass_ref, *work = rest
         now = new_level(pieces[...], level[...])
         level_out[...] = now
     block = BLOCK
     wide = block // LANES
     rows = source.shape[1] // block
-    size = target.shape[1] // block
+    size = mine.shape[1] // block
+    core = place[1]
     for b in range(rows):
-        line = jnp.concatenate(
-            [now[b * wide + part : b * wide + part + 1] for part in range(wide)], axis=1
-        )
+        line = wide_line(now, b * wide)
         here = factors(with_level(source[:, b * block : (b + 1) * block], line), True)
         left[b] = here.astype(F32).T.astype(jnp.bfloat16)
-
-    def build(k, _):
-        at = pl.ds(pl.multiple_of(k * block, block), block)
-        right[k] = factors(with_one(target[:, at]), False)
-        cleared(tops_ref, mass_ref, k)
-        return 0
-
-    lax.fori_loop(0, size, build, 0, unroll=4)
+    for side, points in enumerate((mine, other)):
+
+        def build(k, _, side=side, points=points):
+            at = pl.ds(pl.multiple_of(k * block, block), block)
+            right[side * size + k] = factors(with_one(points[:, at]), False)
+            cleared(tops_ref, mass_ref, side * size + k)
+            return 0
+
+        lax.fori_loop(0, size, build, 0, unroll=4)
 
     def product(row, column, at, chunk):
         return jnp.dot(left[row][at : at + chunk], right[column], preferred_element_type=F32)
 
     half = len(work) // 2
     pair_loop(
-        codes, size, 64, product, lambda row, column: column, tops_ref, mass_ref, work[:half], work[half:]
-    )
-    each = size // out.shape[0]
-
-    def finish(piece, _):
-        for e in range(each):
-            k = piece * each + e
-            at = pl.ds(pl.multiple_of(k * block, block), block)
-            line = joined(tops_ref[k], mass_ref[k]) - SCALE * half_norm(target[:, at])
-            for part in range(wide):
-                out[piece, e * wide + part : e * wide + part + 1, :] = line[
-                    :, part * LANES : (part + 1) * LANES
-                ]
-        return 0
-
-    lax.fori_loop(0, out.shape[0], finish, 0, unroll=4)
-
-
-def combine_kernel(place_ref, pieces, level, out):
-    out[...] = jnp.broadcast_to(new_level(pieces[...], level[place_ref[0]])[None], out.shape)
+        codes, 2 * size, 64, product, lambda row, column: column, tops_ref, mass_ref, work[:half], work[half:]
+    )
+    pieces = out.shape[0] // 2
+    each = size // pieces
+    for side, points in enumerate((mine, other)):
+
+        def finish(piece, _, side=side, points=points):
+            for e in range(each):
+                k = piece * each + e
+                at = pl.ds(pl.multiple_of(k * block, block), block)
+                line = joined(tops_ref[side * size + k], mass_ref[side * size + k])
+                line = line - SCALE * half_norm(points[:, at])
+                for part in range(wide):
+                    out[2 * piece + (core ^ side), e * wide + part : e * wide + part + 1, :] = line[
+                        :, part * LANES : (part + 1) * LANES
+                    ]
+            return 0
+
+        lax.fori_loop(0, pieces, finish, 0, unroll=4)
+
+
+def combine_kernel(place, pieces, level, out, *own):
+    new = new_level(pieces[...], level[place[3]] if own else level[...])
+    out[...] = jnp.broadcast_to(new[None], out.shape)
+    for ref in own:
+        ref[...] = new
 
 
 def last_kernel(pieces, level, out):
@@ -284,51 +320,57 @@
 
 def on_device(source_points, target_points, source_potential, target_potential, neighbours):
     n_row = lax.axis_size("row")
-    n_col = lax.axis_size("col")
+    n_col = lax.axis_size("y") * lax.axis_size("core")
     rows = source_points.shape[1] // BLOCK
     size = target_points.shape[1] // BLOCK
-    col = lax.axis_index("col").astype(jnp.int32).reshape(1)
-    row = lax.axis_index("row").astype(jnp.int32).reshape(1)
+    core = lax.axis_index("core")
+    place = jnp.stack([lax.axis_index("y"), core, size, lax.axis_index("row")]).astype(jnp.int32)
     source_lines = source_points.shape[1] // LANES
     share = target_points.shape[1] // LANES // n_row
     source_level = source_potential.reshape(source_lines, LANES)
     target_level = target_potential.reshape(n_row, share, LANES)
     codes_shape = jax.ShapeDtypeStruct((neighbours.size + LANES,), jnp.int32)
-    column_scratch = scratch((rows, BLOCK, 32), (size, 32, BLOCK), size)
-    row_scratch = scratch((size, 32, BLOCK), (rows, 32, BLOCK), rows)
-    column_out = (n_row, share, LANES)
+    column_scratch = scratch((rows, BLOCK, 32), (2 * size, 32, BLOCK), 2 * size)
+    row_scratch = scratch((2 * size, 32, BLOCK), (rows, 32, BLOCK), rows)
+    column_out = (2 * n_row, share, LANES)
     row_out = (n_col, source_lines, LANES)
-
-    def row_phase(codes, level):
-        return call(row_kernel, row_out, [SMEM, VMEM, VMEM, VMEM], row_scratch)(
-            codes, source_points, target_points, level.reshape(1, -1)
-        )
-
-    def column_level(pieces, level):
-        spread = call(combine_kernel, pieces.shape, [SMEM, VMEM, VMEM], ())(row, pieces, level)
-        return exchanged(spread, "row")
-
-    columns_0, codes = call(
-        functools.partial(column_kernel, True),
-        [column_out, codes_shape],
-        [VMEM, VMEM, VMEM, SMEM, SMEM],
-        column_scratch,
-        60 << 20,
-    )(source_points, target_points, source_level, col, neighbours)
-    column_pieces_0 = exchanged(columns_0, "row")
-    row_pieces_0 = exchanged(row_phase(codes, target_level), "col")
-    target_1 = column_level(column_pieces_0, target_level)
+    both = ("row", "core")
+    across = ("y", "core")
+    swap = [(0, 1), (1, 0)]
+
+    other_points = lax.ppermute(target_points, "core", swap)
+    other_level = lax.ppermute(target_potential, "core", swap)
+    other_points, other_level = lax.optimization_barrier((other_points, other_level))
+    other_level = other_level.reshape(target_level.shape)
+    codes = call(list_kernel, codes_shape, [SMEM, SMEM], ())(place, neighbours)
+    points = (source_points, target_points, other_points)
+
+    def row_phase(levels):
+        later = len(levels) == 1
+        return call(
+            functools.partial(row_kernel, later), row_out, [SMEM, SMEM] + [VMEM] * (3 + len(levels)), row_scratch
+        )(place, codes, *points, *levels)
+
+    columns_0 = call(
+        functools.partial(column_kernel, True), column_out, [SMEM, SMEM] + [VMEM] * 4, column_scratch
+    )(place, codes, *points, source_level)
+    column_pieces_0 = exchanged(columns_0, both)
+    row_pieces_0 = exchanged(row_phase((target_level, other_level)), across)
+    spread_0, mine_1 = call(
+        combine_kernel, [column_out, target_level.shape[1:]], [SMEM, VMEM, VMEM], ()
+    )(place, column_pieces_0, target_level)
+    target_1 = exchanged(spread_0, both).reshape(n_row, 2, share, LANES)
     columns_1, source_1 = call(
         functools.partial(column_kernel, False),
         [column_out, source_level.shape],
-        [VMEM, VMEM, VMEM, SMEM, VMEM],
+        [SMEM, SMEM] + [VMEM] * 5,
         column_scratch,
-    )(source_points, target_points, source_level, codes, row_pieces_0)
-    column_pieces_1 = exchanged(columns_1, "row")
-    rows_1 = row_phase(codes, target_1)
+    )(place, codes, *points, source_level, row_pieces_0)
+    column_pieces_1 = exchanged(columns_1, both)
+    rows_1 = row_phase((target_1,))
     column_pieces_1, rows_1 = lax.optimization_barrier((column_pieces_1, rows_1))
-    row_pieces_1 = exchanged(rows_1, "col")
-    spread = call(combine_kernel, column_out, [SMEM, VMEM, VMEM], ())(row, column_pieces_1, target_1)
+    row_pieces_1 = exchanged(rows_1, across)
+    spread = call(combine_kernel, target_level.shape, [SMEM, VMEM, VMEM], ())(place, column_pieces_1, mine_1)
     target_2 = exchanged(spread, "row")
     source_2 = call(last_kernel, source_level.shape, [VMEM, VMEM], ())(
         row_pieces_1, source_1
@@ -337,7 +379,9 @@
 
 
 def solution(mesh):
-    in_specs = (P(None, "row"), P(None, "col"), P("row"), P("col"), P("row", None))
+    finer = Mesh(mesh.devices.reshape(mesh.shape["row"], -1, 2), ("row", "y", "core"))
+    across = ("y", "core")
+    in_specs = (P(None, "row"), P(None, across), P("row"), P(across), P("row", None))
     return jax.shard_map(
-        on_device, mesh=mesh, in_specs=in_specs, out_specs=(P("row"), P("col")), check_vma=False
-    )
+        on_device, mesh=finer, in_specs=in_specs, out_specs=(P("row"), P(across)), check_vma=False
+    )

time: 121 us -> 132 us (1.091)
  Pallas kernels: 12 us -> 19.1 us
  waiting for transfers between devices: 36.4 us -> 39.3 us
  local copies, waits for them, and re-layouts: 0.66 us -> 2.98 us
  starting transfers between devices: 58.4 us -> 56.9 us
    all_to_all x5, starting transfers between devices: 58.4 us -> 46.2 us  [exchanged(): return lax.all_to_all(array, axis, 0, 0, tiled=True)]
    ppermute x0 -> x2, starting transfers between devices: none -> 10.7 us  [the longest x1 8.75 us: on_device(): other_points = lax.ppermute(target_points, 'core', swap)]
    pallas_call x5 -> x6, Pallas kernels: 8.71 us -> 14.3 us  [the longest x2 6.5 us: row_phase(): call(functools.partial(row_kernel, later), row_out, [SMEM, SMEM] + [VMEM]...]
    all_to_all x5, waiting for transfers between devices: 36.4 us -> 39.3 us  [exchanged(): return lax.all_to_all(array, axis, 0, 0, tiled=True)]
    unnamed x11 -> x15, local copies, waits for them, and re-layouts: 0.66 us -> 2.98 us
    pallas_call x1, Pallas kernels: 2.69 us -> 4.15 us  [on_device(): call(functools.partial(column_kernel, False), [column_out, source_level.s...]
  transfers between devices with their start and end apart: 5 -> 7, of which waited for: 5 -> 5; matrix products, arithmetic and copies ran while one was open for 0% -> 0% of each run, Pallas kernels for 7% -> 10%
where the time goes in v1:
time: 132 us; the launch traced here: 131 us
  starting transfers between devices  56.9 us (43%)
  waiting for transfers between devices  39.3 us (30%)
  Pallas kernels  19.1 us (14%)
  blocking collectives  11.8 us (9%)
  local copies, waits for them, and re-layouts  2.98 us (2%)
    all_to_all x5, starting transfers between devices, exchanged(): return lax.all_to_all(array, axis, 0, 0, tiled=True)  46.2 us
    all_to_all x5, waiting for transfers between devices, exchanged(): return lax.all_to_all(array, axis, 0, 0, tiled=True)  39.3 us
    all_to_all x1, blocking collectives, exchanged(): return lax.all_to_all(array, axis, 0, 0, tiled=True)  11.8 us
    ppermute x1, starting transfers between devices, on_device(): other_points = lax.ppermute(target_points, 'core', swap)  8.75 us
    pallas_call x2, Pallas kernels, row_phase(): call(functools.partial(row_kernel, later), row_out, [SMEM, SMEM] + [VMEM]...  6.5 us
    pallas_call x1, Pallas kernels, on_device(): call(functools.partial(column_kernel, False), [column_out, source_level.s...  4.15 us
    pallas_call x1, Pallas kernels, on_device(): call(functools.partial(column_kernel, True), column_out, [SMEM, SMEM] + [...  4.09 us
    unnamed x15, local copies, waits for them, and re-layouts  2.98 us
  transfers between devices with their start and end apart: 7, of which 5 were waited for; matrix products, arithmetic and copies ran while one was open for 0% of the time, Pallas kernels for 10%

profile of v1, /device:TPU:1, one launch (start us, length us, event | category | flops | bytes accessed | tf_op | source)
XLA Modules:
  0.0 130.9 jit_solution(9235900342961462942)
XLA Ops:
  0.6 0.0 copy-start.2
  0.6 8.7 %collective-permute-start = (f32[3,16384]{1,0:T(4,128)}, f32[3,16384]{1,0:T(4,128)S(1)}, u32[]{:S(2)}, u32[]{:S(2)}) collective-permute-start(f32[3,16384]{1,0:T(4,128)} %mine.7), channel_id=1, source_target_pairs={{0,1},{1,0},{2,3},{3,2},{4,5},{5,4},{6,7},{7,6},{8,9},{9,8},{10,11... | collective-permute-start | bytes 589832 | tf_op jit(solution)/shard_map/ppermute | solution.py:341
  9.4 1.9 %collective-permute-start.1 = (f32[16384]{0:T(1024)}, f32[16384]{0:T(1024)S(1)}, u32[]{:S(2)}, u32[]{:S(2)}) collective-permute-start(f32[16384]{0:T(1024)} %param.8), channel_id=1, source_target_pairs={{0,1},{1,0},{2,3},{3,2},{4,5},{5,4},{6,7},{7,6},{8,9},{9,8},{10,11... | collective-permute-start | bytes 196616 | tf_op jit(solution)/shard_map/ppermute | solution.py:342
  11.3 0.1 pad_add_fusion.place
  11.4 0.0 copy-start.6
  11.4 0.7 copy-done.6
  12.1 1.7 %shard_map.68.codes = s32[640]{0:T(1024)S(1)} custom-call(s32[4]{0:T(128)S(1)} %pad_add_fusion.place, s32[8,64]{1,0:T(8,128)S(1)} %copy-done.6), custom_call_target="tpu_custom_call" | custom-call | tf_op jit(solution)/shard_map/pallas_call | solution.py:345
  13.8 0.0 collective-permute-done.1
  13.9 0.0 collective-permute-done.other
  13.9 0.0 copy-done.2
  13.9 0.0 copy-start
  13.9 0.9 copy-done
  14.8 0.0 copy-start.4
  14.8 0.7 copy-done.4
  15.5 0.0 copy-start.3
  15.5 4.1 %shard_map.71 = f32[64,4,128]{2,1,0:T(4,128)} custom-call(s32[4]{0:T(128)S(1)} %pad_add_fusion.place, s32[640]{0:T(1024)S(1)} %shard_map.68.codes, f32[3,2048]{1,0:T(4,128)S(1)} %copy-done.2, f32[3,16384]{1,0:T(4,128)S(1)} %copy-done, f32[3,16384]{1,0:T(4,128)S(1)} %collective-permute-done.other, f32[16,128]{1,0:T(8,128)S(1)} %bitcast.13), custom_call_target="tpu_custom_call" | custom-call | tf_op jit(solution)/shard_map/pallas_call | solution.py:354
  19.6 0.0 copy-start.1
  19.6 8.1 %all-to-all-start.2 = ((f32[64,4,128]{2,1,0:T(4,128)}), f32[64,4,128]{2,1,0:T(4,128)S(1)}, u32[]{:S(2)}, u32[]{:S(2)}) async-start(f32[64,4,128]{2,1,0:T(4,128)} %shard_map.71), calls=%async_computation.2 | async-start | bytes 262144 | tf_op jit(solution)/shard_map/all_to_all | solution.py:318
  27.7 0.0 copy-done.3
  27.7 0.0 copy-done.1
  27.7 3.2 %shard_map.69 = f32[16,16,128]{2,1,0:T(8,128)} custom-call(s32[4]{0:T(128)S(1)} %pad_add_fusion.place, s32[640]{0:T(1024)S(1)} %shard_map.68.codes, f32[3,2048]{1,0:T(4,128)S(1)} %copy-done.2, f32[3,16384]{1,0:T(4,128)S(1)} %copy-done.1, f32[3,16384]{1,0:T(4,128)S(1)} %collective-permute-done.other, f32[32,4,128]{2,1,0:T(4,128)S(1)} %bitcast.10, ...), custom_call_target="tpu_custom_call" | custom-call | tf_op jit(solution)/shard_map/pallas_call | solution.py:350
  31.0 7.8 %all-to-all-done.2.pieces = f32[64,4,128]{2,1,0:T(4,128)S(1)} async-done(((f32[64,4,128]{2,1,0:T(4,128)}), f32[64,4,128]{2,1,0:T(4,128)S(1)}, u32[]{:S(2)}, u32[]{:S(2)}) %all-to-all-start.2) | async-done | bytes 131104 | tf_op jit(solution)/shard_map/all_to_all | solution.py:318
  38.8 13.1 %all-to-all-start = ((f32[16,16,128]{2,1,0:T(8,128)}), f32[16,16,128]{2,1,0:T(8,128)S(1)}, u32[]{:S(2)}, u32[]{:S(2)}) async-start(f32[16,16,128]{2,1,0:T(8,128)} %shard_map.69), calls=%async_computation | async-start | bytes 262144 | tf_op jit(solution)/shard_map/all_to_all | solution.py:318
  51.9 1.3 %shard_map.72 = (f32[64,4,128]{2,1,0:T(4,128)}, f32[4,128]{1,0:T(4,128)S(1)}) custom-call(s32[4]{0:T(128)S(1)} %pad_add_fusion.place, f32[64,4,128]{2,1,0:T(4,128)S(1)} %all-to-all-done.2.pieces, f32[32,4,128]{2,1,0:T(4,128)S(1)} %bitcast.11), custom_call_target="tpu_custom_call" | custom-call | tf_op jit(solution)/shard_map/pallas_call | solution.py:359
  53.2 7.6 %all-to-all-done.rest_0_ = f32[16,16,128]{2,1,0:T(8,128)S(1)} async-done(((f32[16,16,128]{2,1,0:T(8,128)}), f32[16,16,128]{2,1,0:T(8,128)S(1)}, u32[]{:S(2)}, u32[]{:S(2)}) %all-to-all-start) | async-done | bytes 131104 | tf_op jit(solution)/shard_map/all_to_all | solution.py:318
  60.8 0.0 copy-start.5
  60.8 8.4 %all-to-all-start.3 = ((f32[64,4,128]{2,1,0:T(4,128)}), f32[64,4,128]{2,1,0:T(4,128)S(1)}, u32[]{:S(2)}, u32[]{:S(2)}) async-start(f32[64,4,128]{2,1,0:T(4,128)} %get-tuple-element.13), calls=%async_computation.3 | async-start | bytes 262144 | tf_op jit(solution)/shard_map/all_to_all | solution.py:318
  69.2 0.0 copy-done.5
  69.2 4.1 %shard_map.70 = (f32[64,4,128]{2,1,0:T(4,128)}, f32[16,128]{1,0:T(8,128)S(1)}) custom-call(s32[4]{0:T(128)S(1)} %pad_add_fusion.place, s32[640]{0:T(1024)S(1)} %shard_map.68.codes, f32[3,2048]{1,0:T(4,128)S(1)} %copy-done.2, f32[3,16384]{1,0:T(4,128)S(1)} %copy-done.1, f32[3,16384]{1,0:T(4,128)S(1)} %collective-permute-done.other, f32[16,128]{1,0:T(8,128)S(1)} %bitcast.14, ...), custom_call_target="tpu_custom_call" | custom-call | tf_op jit(solution)/shard_map/pallas_call | solution.py:363
  73.4 6.9 %all-to-all-done.3 = f32[64,4,128]{2,1,0:T(4,128)S(1)} async-done(((f32[64,4,128]{2,1,0:T(4,128)}), f32[64,4,128]{2,1,0:T(4,128)S(1)}, u32[]{:S(2)}, u32[]{:S(2)}) %all-to-all-start.3) | async-done | bytes 131104 | tf_op jit(solution)/shard_map/all_to_all | solution.py:318
  80.3 4.4 %all-to-all-start.1 = ((f32[64,4,128]{2,1,0:T(4,128)}), f32[64,4,128]{2,1,0:T(4,128)S(1)}, u32[]{:S(2)}, u32[]{:S(2)}) async-start(f32[64,4,128]{2,1,0:T(4,128)} %get-tuple-element.12), calls=%async_computation.1 | async-start | bytes 262144 | tf_op jit(solution)/shard_map/all_to_all | solution.py:318
  84.8 3.2 %shard_map.73 = f32[16,16,128]{2,1,0:T(8,128)} custom-call(s32[4]{0:T(128)S(1)} %pad_add_fusion.place, s32[640]{0:T(1024)S(1)} %shard_map.68.codes, f32[3,2048]{1,0:T(4,128)S(1)} %copy-done.2, f32[3,16384]{1,0:T(4,128)S(1)} %copy-done.1, f32[3,16384]{1,0:T(4,128)S(1)} %collective-permute-done.other, f32[32,2,4,128]{3,2,1,0:T(4,128)S(1)} %bitcast.9), custom_call_target="tpu_custom_call" | custom-call | tf_op jit(solution)/shard_map/pallas_call | solution.py:350
  88.0 8.1 %all-to-all-done.1.pieces = f32[64,4,128]{2,1,0:T(4,128)S(1)} async-done(((f32[64,4,128]{2,1,0:T(4,128)}), f32[64,4,128]{2,1,0:T(4,128)S(1)}, u32[]{:S(2)}, u32[]{:S(2)}) %all-to-all-start.1) | async-done | bytes 131104 | tf_op jit(solution)/shard_map/all_to_all | solution.py:318
  96.1 0.7 shard_map.75
  96.7 11.8 %all_to_all.30 = f32[32,4,128]{2,1,0:T(4,128)S(1)} all-to-all(f32[32,4,128]{2,1,0:T(4,128)S(1)} %shard_map.75), channel_id=1, replica_groups=mesh['row'=32,'y'=8,'core'=2] {'row'}, dimensions={0} | all-to-all | bytes 131072 | tf_op jit(solution)/shard_map/all_to_all | solution.py:318
  108.6 12.2 %all-to-all-start.4 = ((f32[16,16,128]{2,1,0:T(8,128)}), f32[16,16,128]{2,1,0:T(8,128)S(1)}, u32[]{:S(2)}, u32[]{:S(2)}) async-start(f32[16,16,128]{2,1,0:T(8,128)} %shard_map.73), calls=%async_computation.4 | async-start | bytes 262144 | tf_op jit(solution)/shard_map/all_to_all | solution.py:318
  120.8 8.9 %all-to-all-done.4.pieces = f32[16,16,128]{2,1,0:T(8,128)S(1)} async-done(((f32[16,16,128]{2,1,0:T(8,128)}), f32[16,16,128]{2,1,0:T(8,128)S(1)}, u32[]{:S(2)}, u32[]{:S(2)}) %all-to-all-start.4) | async-done | bytes 131104 | tf_op jit(solution)/shard_map/all_to_all | solution.py:318
  129.6 0.6 shard_map.74
  130.3 0.6 copy.8
Async XLA Ops:
  0.6 13.2 %copy-start.2 = (f32[3,2048]{1,0:T(4,128)S(1)}, f32[3,2048]{1,0:T(4,128)}, u32[]{:S(2)}) copy-start(f32[3,2048]{1,0:T(4,128)} %source.7) | copy-start | bytes 73732
  0.6 13.2 %collective-permute-start = (f32[3,16384]{1,0:T(4,128)}, f32[3,16384]{1,0:T(4,128)S(1)}, u32[]{:S(2)}, u32[]{:S(2)}) collective-permute-start(f32[3,16384]{1,0:T(4,128)} %mine.7), channel_id=1, source_target_pairs={{0,1},{1,0},{2,3},{3,2},{4,5},{5,4},{6,7},{7,6},{8,9},{9,8},{10,11... | collective-permute-start | bytes 589832 | tf_op jit(solution)/shard_map/ppermute | solution.py:341
  9.4 4.5 %collective-permute-start.1 = (f32[16384]{0:T(1024)}, f32[16384]{0:T(1024)S(1)}, u32[]{:S(2)}, u32[]{:S(2)}) collective-permute-start(f32[16384]{0:T(1024)} %param.8), channel_id=1, source_target_pairs={{0,1},{1,0},{2,3},{3,2},{4,5},{5,4},{6,7},{7,6},{8,9},{9,8},{10,11... | collective-permute-start | bytes 196616 | tf_op jit(solution)/shard_map/ppermute | solution.py:342
  11.4 0.7 copy-start.6
  13.9 1.0 copy-start
  14.8 0.7 copy-start.4
  15.5 12.2 %copy-start.3 = (f32[16384]{0:T(1024)S(1)}, f32[16384]{0:T(1024)}, u32[]{:S(2)}) copy-start(f32[16384]{0:T(1024)} %param.8) | copy-start | bytes 196612
  19.6 8.1 %copy-start.1 = (f32[3,16384]{1,0:T(4,128)S(1)}, f32[3,16384]{1,0:T(4,128)}, u32[]{:S(2)}) copy-start(f32[3,16384]{1,0:T(4,128)} %mine.7) | copy-start | bytes 589828
  19.6 19.2 %all-to-all-start.2 = ((f32[64,4,128]{2,1,0:T(4,128)}), f32[64,4,128]{2,1,0:T(4,128)S(1)}, u32[]{:S(2)}, u32[]{:S(2)}) async-start(f32[64,4,128]{2,1,0:T(4,128)} %shard_map.71), calls=%async_computation.2 | async-start | bytes 262144 | tf_op jit(solution)/shard_map/all_to_all | solution.py:318
  38.8 22.0 %all-to-all-start = ((f32[16,16,128]{2,1,0:T(8,128)}), f32[16,16,128]{2,1,0:T(8,128)S(1)}, u32[]{:S(2)}, u32[]{:S(2)}) async-start(f32[16,16,128]{2,1,0:T(8,128)} %shard_map.69), calls=%async_computation | async-start | bytes 262144 | tf_op jit(solution)/shard_map/all_to_all | solution.py:318
  60.8 8.4 %copy-start.5 = (f32[2048]{0:T(1024)S(1)}, f32[2048]{0:T(1024)}, u32[]{:S(2)}) copy-start(f32[2048]{0:T(1024)} %param.7) | copy-start | bytes 24580
  60.8 19.5 %all-to-all-start.3 = ((f32[64,4,128]{2,1,0:T(4,128)}), f32[64,4,128]{2,1,0:T(4,128)S(1)}, u32[]{:S(2)}, u32[]{:S(2)}) async-start(f32[64,4,128]{2,1,0:T(4,128)} %get-tuple-element.13), calls=%async_computation.3 | async-start | bytes 262144 | tf_op jit(solution)/shard_map/all_to_all | solution.py:318
  80.3 15.8 %all-to-all-start.1 = ((f32[64,4,128]{2,1,0:T(4,128)}), f32[64,4,128]{2,1,0:T(4,128)S(1)}, u32[]{:S(2)}, u32[]{:S(2)}) async-start(f32[64,4,128]{2,1,0:T(4,128)} %get-tuple-element.12), calls=%async_computation.1 | async-start | bytes 262144 | tf_op jit(solution)/shard_map/all_to_all | solution.py:318
  108.6 21.1 %all-to-all-start.4 = ((f32[16,16,128]{2,1,0:T(8,128)}), f32[16,16,128]{2,1,0:T(8,128)S(1)}, u32[]{:S(2)}, u32[]{:S(2)}) async-start(f32[16,16,128]{2,1,0:T(8,128)} %shard_map.73), calls=%async_computation.4 | async-start | bytes 262144 | tf_op jit(solution)/shard_map/all_to_all | solution.py:318
